TPU v7x, 32 devices: a whole 2x2x4 slice. The times are simulated.
32 devices in a mesh: groups: 2 (over y), ctx: 4 (over z), head: 2 (over x), sub: 2 (over core).
Axes of the slice: x: 2, y: 2, z: 4, core: 2. Of those that a mesh axis runs over, the one named last changes fastest.
Arguments:
- hidden_in: bfloat16 [1024, 5120], P(('groups', 'ctx'), 'sub'), parts along dimension 0, may hold values from -6 to 6
- w_qkv: bfloat16 [5120, 8, 896], P('sub', 'head', 'ctx'), may hold values from -0.078125 to 0.078125
- qkv_bias: bfloat16 [8, 896], P('head'), may hold values from -3 to 3
- w_out: bfloat16 [8, 640, 5120], P('head', 'ctx'), may hold values from -0.078125 to 0.078125
- prev_keys: bfloat16 [1024, 8, 128], P(('groups', 'ctx', 'sub'), 'head'), parts along dimension 0, may hold values from -60 to 60
- prev_values: bfloat16 [1024, 8, 128], P(('groups', 'ctx', 'sub'), 'head'), parts along dimension 0, may hold values from -6 to 6
- shard_blocks: int32 [8], P('groups'), parts along dimension 0, may hold values from 0 to 3, each once
Outputs:
- attn_out: bfloat16 [1024, 5120], P(('groups', 'ctx', 'sub'), 'head'), parts along dimension 0
There are 2 independent parts, one for each index of `groups`. A program takes and returns all parts, laid end to end along the dimension named above; an argument that names none is the same for every part. Nothing has to cross between parts.
Inputs may be any that keep to these rules, and one draw needn't show every extreme that they name: Index c of ctx holds the positions shard_blocks[c] * 128 to shard_blocks[c] * 128 + 127; every block occurs once.
All inputs are finite; a program needn't handle non-finite values.
Results may differ from a plain program's by a relative error of at most 0.015.
The roundings to bfloat16 on the way count: a program that leaves them out, or rounds other values in their place, can miss the bound.
Values may be sent and summed in bfloat16 or wider, within the bound.
No kernel may reach another device: no remote copies, remote signals or barrier semaphores. Data moves between devices by JAX's collectives and lax.ppermute only.
A program may use at most 64 MiB of HBM per device.

v0:
```python
import math
import jax
import jax.numpy as jnp
from jax import lax
from jax.sharding import PartitionSpec as P

G = 5
HD = 128
NPREV = 2
rope_base = 10000000.0
neg_big = -1e30


def rotate(vectors, positions):
    half_width = vectors.shape[-1] // 2
    frequency = rope_base ** (
        -(jnp.arange(half_width, dtype=jnp.float32) * 2.0) / vectors.shape[-1]
    )
    angles = positions.astype(jnp.float32)[:, None] * frequency[None, :]
    extra = (1,) * (vectors.ndim - 2)
    cosine = jnp.cos(angles).reshape((angles.shape[0],) + extra + (half_width,))
    sine_part = jnp.sin(angles).reshape((angles.shape[0],) + extra + (half_width,))
    first = vectors[..., :half_width]
    second = vectors[..., half_width:]
    return jnp.concatenate(
        [first * cosine - second * sine_part, second * cosine + first * sine_part], axis=-1
    )


def lookup(small_table, wanted):
    entries = jnp.arange(small_table.shape[0], dtype=jnp.int32)
    return jnp.sum(jnp.where(wanted[..., None] == entries, small_table, 0), axis=-1)


def local(hidden_in, w_qkv, qkv_bias, w_out, prev_keys, prev_values, shard_blocks):
    n_ctx = lax.axis_size("ctx")
    n_sub = lax.axis_size("sub")
    n_head = lax.axis_size("head")
    tok_ctx = hidden_in.shape[0]
    tok_dev = tok_ctx // n_sub
    span_len = tok_ctx * n_ctx // 2
    kv_dev = w_qkv.shape[1]
    me_ctx = lax.axis_index("ctx")
    me_sub = lax.axis_index("sub")
    partial_value = jnp.einsum(
        "td,dhn->thn",
        hidden_in,
        lax.all_gather(w_qkv, "ctx", axis=2, tiled=True),
        preferred_element_type=jnp.float32,
    )
    joined = lax.psum_scatter(partial_value, "sub", scatter_dimension=0, tiled=True)
    joined = (joined + qkv_bias.astype(jnp.float32)[None]).reshape(tok_dev, kv_dev, G + 2, HD)
    owner_block = lookup(shard_blocks, me_ctx)
    positions = owner_block * tok_ctx + me_sub * tok_dev + jnp.arange(tok_dev, dtype=jnp.int32)
    span_q = NPREV + positions // span_len
    local_q = positions % span_len
    queries = joined[:, :, :G]

    def arrange(rotated):
        return jnp.transpose(rotated.astype(jnp.bfloat16), (1, 0, 2, 3)).reshape(
            kv_dev, tok_dev * G, HD
        )

    q_intra = arrange(rotate(queries, local_q))
    q_succ = arrange(rotate(queries, local_q + span_len))
    q_inter = arrange(rotate(queries, jnp.full((tok_dev,), 2 * span_len - 1, jnp.int32)))
    k_cur = rotate(joined[:, :, G], local_q).astype(jnp.bfloat16)
    v_cur = joined[:, :, G + 1].astype(jnp.bfloat16)
    old_rows = (me_ctx * n_sub + me_sub) * tok_dev + jnp.arange(tok_dev, dtype=jnp.int32)
    k_prev = rotate(prev_keys.astype(jnp.float32), old_rows % span_len).astype(jnp.bfloat16)
    row_span = jnp.repeat(span_q, G)
    row_local = jnp.repeat(local_q, G)
    own_span = span_q[0]
    score_scale = HD ** (-0.5)
    row_count = tok_dev * G
    start_state = (
        jnp.full((kv_dev, row_count), neg_big, jnp.float32),
        jnp.zeros((kv_dev, row_count), jnp.float32),
        jnp.zeros((kv_dev, row_count, HD), jnp.float32),
    )

    def scores_of(query_set, key_block):
        return (
            jnp.einsum("hrd,khd->hrk", query_set, key_block, preferred_element_type=jnp.float32)
            * score_scale
        )

    def update(running, scores, allowed, value_block):
        running_max, weight_sum, weighted = running
        block_max = jnp.max(jnp.where(allowed, scores, neg_big), axis=2)
        new_max = jnp.maximum(running_max, block_max)
        weights = jnp.where(allowed, jnp.exp(scores - new_max[..., None]), 0.0)
        rescale = jnp.exp(running_max - new_max)
        weight_sum = weight_sum * rescale + jnp.sum(weights, axis=2)
        weighted = weighted * rescale[..., None] + jnp.einsum(
            "hrk,khd->hrd",
            weights.astype(jnp.bfloat16),
            value_block,
            preferred_element_type=jnp.float32,
        )
        return (new_max, weight_sum, weighted)

    def current_block(running, key_block, value_block, key_index):
        shard_index = key_index // tok_dev
        key_pos = (
            lookup(shard_blocks, shard_index // n_sub) * tok_ctx
            + shard_index % n_sub * tok_dev
            + key_index % tok_dev
        )
        key_span = NPREV + key_pos // span_len
        key_local = key_pos % span_len
        same_span = key_span[None, :] == row_span[:, None]
        before = key_span[None, :] == row_span[:, None] - 1
        allowed = same_span & (key_local[None, :] <= row_local[:, None]) | before
        query_set = jnp.where(key_span[0] == own_span, q_intra, q_succ)
        return update(running, scores_of(query_set, key_block), allowed[None], value_block)

    def earlier_block(running, key_block, value_block, key_index):
        block_span = key_index[0] // span_len
        query_set = jnp.where(block_span == own_span - 1, q_succ, q_inter)
        scores = scores_of(query_set, key_block)
        return update(running, scores, jnp.ones(scores.shape, jnp.bool_), value_block)

    cur_keys = lax.all_gather(k_cur, ("ctx", "sub"), axis=0, tiled=True)
    cur_values = lax.all_gather(v_cur, ("ctx", "sub"), axis=0, tiled=True)
    old_keys = lax.all_gather(k_prev, ("ctx", "sub"), axis=0, tiled=True)
    old_values = lax.all_gather(prev_values, ("ctx", "sub"), axis=0, tiled=True)
    piece_rows = cur_keys.shape[0]
    block_rows = math.gcd(piece_rows, tok_dev)

    def turn(turn_index, state_in):
        offset = turn_index * block_rows
        key_index = offset + jnp.arange(block_rows, dtype=jnp.int32)

        def take(values):
            return lax.dynamic_slice_in_dim(values, offset, block_rows, 0)

        state_in = current_block(state_in, take(cur_keys), take(cur_values), key_index)
        return earlier_block(state_in, take(old_keys), take(old_values), key_index)

    running_max, weight_sum, weighted = lax.fori_loop(
        0, piece_rows // block_rows, turn, start_state
    )
    head_out = (weighted / weight_sum[..., None]).astype(jnp.bfloat16)
    head_out = jnp.transpose(head_out.reshape(kv_dev, tok_dev, G, HD), (1, 0, 2, 3)).reshape(
        tok_dev, kv_dev, G * HD
    )
    group_cols = w_out.shape[2] // (n_head * n_sub)
    split_cols = w_out.reshape(kv_dev, w_out.shape[1], n_head, n_sub, group_cols)
    own_cols = lax.dynamic_index_in_dim(split_cols, me_sub, 3, keepdims=False).reshape(
        kv_dev, w_out.shape[1], n_head * group_cols
    )
    pair_heads = lax.all_gather(head_out, "sub", axis=0, tiled=True)
    summed = jnp.einsum(
        "thn,hnd->td",
        pair_heads,
        lax.all_gather(own_cols, "ctx", axis=1, tiled=True),
        preferred_element_type=jnp.float32,
    )
    shares = lax.psum_scatter(summed.astype(jnp.bfloat16), "head", scatter_dimension=1, tiled=True)
    return lax.all_to_all(shares, "sub", split_axis=0, concat_axis=1, tiled=True)


def solution(mesh):
    return jax.shard_map(
        local,
        mesh=mesh,
        in_specs=(
            P(("groups", "ctx"), "sub"),
            P("sub", "head", "ctx"),
            P("head", None),
            P("head", "ctx", None),
            P(("groups", "ctx", "sub"), "head", None),
            P(("groups", "ctx", "sub"), "head", None),
            P("groups"),
        ),
        out_specs=P(("groups", "ctx", "sub"), "head"),
        check_vma=False,
    )
```

profile of v0, /device:TPU:0, one launch (start us, length us, event | category | flops | bytes accessed | tf_op | source)
XLA Modules:
  0.0 695.2 jit_solution(7797207133418223826)
XLA Ops:
  6.5 0.7 all-gather.4.cloned.1.call-update
  7.3 317.9 %all-gather.4.cloned.1.call-done = bf16[2560,4,896]{0,2,1:T(8,128)(2,1)} async-done(((bf16[2560,4,224]{0,2,1:T(8,128)(2,1)}), bf16[2560,4,896]{0,2,1:T(8,128)(2,1)}) %all-gather.4.cloned.1.call-update) | async-done | bytes 18350096 | tf_op jit(solution)/shard_map/all_gather | solution.py:48
  325.2 13.3 %fusion.36 = f32[128,4,896]{2,0,1:T(8,128)} fusion(bf16[2560,4,896]{0,2,1:T(8,128)(2,1)} %all-gather.4.cloned.1.call-done, bf16[128,2560]{1,0:T(8,128)(2,1)S(1)} %copy-done), kind=kOutput, calls=%fused_computation.72 | convolution fusion | flops 2348810240 | bytes 20840448 | tf_op jit(solution)/shard_map/td,dhn->thn/dot_general | solution.py:45
  338.5 0.2 all-gather.6.cloned.1.call-start
  338.8 15.2 %reshape.509 = bf16[4,160,2,2,1280]{4,3,2,1,0:T(2,128)(2,1)} reshape(bf16[4,160,5120]{2,1,0:T(8,128)(2,1)} %param.12) | data formatting | bytes 13107200 | tf_op jit(solution)/shard_map/reshape | solution.py:149
  354.0 55.3 %dynamic-slice_reduce_fusion = bf16[4,160,2,1280]{3,2,1,0:T(2,128)(2,1)} fusion(bf16[4,160,2,2,1280]{4,3,2,1,0:T(2,128)(2,1)} %reshape.509, s32[]{:T(128)S(6)} %select_n.317), kind=kLoop, calls=%fused_computation.63 | loop fusion | bytes 6553604 | tf_op jit(solution)/shard_map/jit(dynamic_index_in_dim)/dynamic_slice | solution.py:150
  409.3 8.2 %reshape.510 = bf16[4,160,2560]{2,1,0:T(8,128)(2,1)} reshape(bf16[4,160,2,1280]{3,2,1,0:T(2,128)(2,1)} %dynamic-slice_reduce_fusion) | data formatting | bytes 6553600 | tf_op jit(solution)/shard_map/reshape | solution.py:150
  417.7 0.6 fusion.38
  419.1 0.4 multiply_cosine_fusion
  419.7 16.1 %all_gather.23 = bf16[512,4,128]{2,0,1:T(8,128)(2,1)S(1)} all-gather(bf16[64,4,128]{2,0,1:T(8,128)(2,1)S(1)} %pad_maximum_fusion.1), channel_id=1, replica_groups=mesh['groups'=2,'ctx'=4,'head'=2,'sub'=2] {'ctx','sub'}, dimensions={0}, use_global_device_ids=true | all-gather | bytes 589824 | tf_op jit(solution)/shard_map/all_gather | solution.py:126
  435.9 26.1 %all_gather.25 = bf16[512,4,128]{2,0,1:T(8,128)(2,1)} all-gather(bf16[64,4,128]{2,0,1:T(8,128)(2,1)S(1)} %copy.42), channel_id=1, replica_groups=mesh['groups'=2,'ctx'=4,'head'=2,'sub'=2] {'ctx','sub'}, dimensions={0}, use_global_device_ids=true | all-gather | bytes 589824 | tf_op jit(solution)/shard_map/all_gather | solution.py:127
  462.0 1.2 broadcast_add_fusion.1
  463.9 30.2 %all_gather.22 = bf16[512,4,128]{2,0,1:T(8,128)(2,1)} all-gather(bf16[64,4,128]{2,0,1:T(8,128)(2,1)S(1)} %pad_maximum_fusion), channel_id=1, replica_groups=mesh['groups'=2,'ctx'=4,'head'=2,'sub'=2] {'ctx','sub'}, dimensions={0}, use_global_device_ids=true | all-gather | bytes 589824 | tf_op jit(solution)/shard_map/all_gather | solution.py:124
  494.1 27.9 %all-gather = bf16[512,4,1,128]{3,2,0,1:T(2,128)(2,1)S(1)} all-gather(bf16[64,4,1,128]{3,2,0,1:T(2,128)(2,1)S(1)} %slice.97), channel_id=2, replica_groups=mesh['groups'=2,'ctx'=4,'head'=2,'sub'=2] {'ctx','sub'}, dimensions={0}, use_global_device_ids=true | all-gather | bytes 589824 | tf_op jit(solution)/shard_map/all_gather | solution.py:125
  522.0 1.1 subtract_convert_fusion
  523.2 0.4 maximum_bitcast_fusion.2
  523.5 0.4 copy.40
  524.0 0.4 maximum_bitcast_fusion.1
  524.4 0.4 copy.39
  524.9 0.4 maximum_bitcast_fusion
  525.2 0.4 copy.38
  525.7 34.2 %while.21 = (s32[]{:T(128)}, f32[4,320]{1,0:T(4,128)S(1)}, f32[4,320]{1,0:T(4,128)S(1)}, f32[4,320,128]{2,1,0:T(8,128)S(1)}, s32[4]{0:T(128)S(1)}, /*index=5*/s3...) while((s32[]{:T(128)}, f32[4,320]{1,0:T(4,128)S(1)}, ...), condition=%wide.region_8.9_spmd.clone, body=%wide.region_2.8_spmd.clone.sunk | while | flops 86380112 | bytes 6466017 | solution.py:141
  526.7 1.1 select_reduce_fusion.5
  527.8 0.3 fusion.64
  528.3 0.6 fusion.70
  528.8 1.2 convolution_add_fusion.3
  530.7 0.1 eq.213
  530.9 1.1 select_reduce_fusion.5
  532.0 0.3 fusion.64
  532.5 0.6 fusion.70
  533.1 1.2 convolution_add_fusion.3
  535.2 1.1 select_reduce_fusion.5
  536.3 0.3 fusion.64
  536.8 0.6 fusion.70
  537.4 1.2 convolution_add_fusion.3
  539.5 1.1 select_reduce_fusion.5
  540.6 0.3 fusion.64
  541.1 0.6 fusion.70
  541.7 1.2 convolution_add_fusion.3
  543.8 1.1 select_reduce_fusion.5
  544.9 0.3 fusion.64
  545.4 0.6 fusion.70
  545.9 1.2 convolution_add_fusion.3
  548.0 1.1 select_reduce_fusion.5
  549.2 0.3 fusion.64
  549.7 0.6 fusion.70
  550.2 1.2 convolution_add_fusion.3
  552.3 1.1 select_reduce_fusion.5
  553.4 0.3 fusion.64
  553.9 0.6 fusion.70
  554.5 1.2 convolution_add_fusion.3
  556.6 1.1 select_reduce_fusion.5
  557.7 0.3 fusion.64
  558.2 0.6 fusion.70
  558.8 1.2 convolution_add_fusion.3
  560.0 0.2 divide_convert_fusion
  560.2 0.3 copy.46
  560.6 0.4 reshape.508
  561.0 2.4 all_gather.26
  563.4 96.7 %all-gather.6.cloned.1.call-done = bf16[4,640,2560]{2,1,0:T(8,128)(2,1)} async-done(((bf16[4,160,2560]{2,1,0:T(8,128)(2,1)}), bf16[4,640,2560]{2,1,0:T(8,128)(2,1)}) %all-gather.6.cloned.1.call-update) | async-done | bytes 13107216 | tf_op jit(solution)/shard_map/all_gather | solution.py:157
  660.1 7.5 %fusion.35 = bf16[128,2560]{1,0:T(8,128)(2,1)} fusion(bf16[128,4,640]{2,0,1:T(8,128)(2,1)S(1)} %all_gather.26, bf16[4,640,2560]{2,1,0:T(8,128)(2,1)} %all-gather.6.cloned.1.call-done), kind=kOutput, calls=%fused_computation.65 | convolution fusion | flops 1678049280 | bytes 14417920 | tf_op jit(solution)/shard_map/thn,hnd->td/dot_general | solution.py:154
  667.6 15.3 %reduce-scatter.5.cloned.1.call-done = bf16[128,1280]{1,0:T(8,128)(2,1)} async-done(((bf16[128,2560]{1,0:T(8,128)(2,1)}), bf16[128,1280]{1,0:T(8,128)(2,1)}) %reduce-scatter.5.cloned.1.call-update) | async-done | bytes 327696 | tf_op jit(solution)/shard_map/reduce_scatter | solution.py:160
  682.9 5.0 all_to_all.19
  687.9 0.7 copy.52
  (161 shorter events, 8.4 us)
Async XLA Ops:
  6.5 318.6 %copy-start = (bf16[128,2560]{1,0:T(8,128)(2,1)S(1)}, bf16[128,2560]{1,0:T(8,128)(2,1)}, u32[]{:S(2)}) copy-start(bf16[128,2560]{1,0:T(8,128)(2,1)} %param.9) | copy-start | bytes 1966084
  6.5 318.6 %all-gather.4.cloned.1.call-start = ((), (), s32[]{:S(2)}) async-start(), calls=%async_computation.3 | async-start | bytes 22937600 | tf_op jit(solution)/shard_map/all_gather | solution.py:48
  7.3 454.7 %reduce-scatter.3.cloned.1.call-start = ((), (), s32[]{:S(2)}) async-start(), calls=%async_computation.4 | async-start | bytes 2752512 | tf_op jit(solution)/shard_map/reduce_scatter | solution.py:51
  338.5 321.5 %all-gather.6.cloned.1.call-start = ((), (), s32[]{:S(2)}) async-start(), calls=%async_computation.5 | async-start | bytes 16384000 | tf_op jit(solution)/shard_map/all_gather | solution.py:157
  409.3 8.3 %copy-start.5 = (s32[4]{0:T(128)S(1)}, s32[4]{0:T(128)}, u32[]{:S(2)}) copy-start(s32[4]{0:T(128)} %param.15) | copy-start | bytes 52
  409.3 9.7 %copy-start.4 = (bf16[4,896]{1,0:T(4,128)(2,1)S(1)}, bf16[4,896]{1,0:T(4,128)(2,1)}, u32[]{:S(2)}) copy-start(bf16[4,896]{1,0:T(4,128)(2,1)} %param.11) | copy-start | bytes 21508
  409.3 9.7 %copy-start.3 = (bf16[64,4,128]{2,1,0:T(4,128)(2,1)S(1)}, bf16[64,4,128]{2,1,0:T(4,128)(2,1)}, u32[]{:S(2)}) copy-start(bf16[64,4,128]{2,1,0:T(4,128)(2,1)} %param.14) | copy-start | bytes 196612
  409.3 9.7 %copy-start.2 = (bf16[64,4,128]{2,1,0:T(4,128)(2,1)S(1)}, bf16[64,4,128]{2,1,0:T(4,128)(2,1)}, u32[]{:S(2)}) copy-start(bf16[64,4,128]{2,1,0:T(4,128)(2,1)} %param.13) | copy-start | bytes 196612
  417.6 265.3 %reduce-scatter.5.cloned.1.call-start = ((), (), s32[]{:S(2)}) async-start(), calls=%async_computation.6 | async-start | bytes 983040 | tf_op jit(solution)/shard_map/reduce_scatter | solution.py:160
  561.0 127.7 %copy-start.1 = (bf16[128,2560]{1,0:T(8,128)(2,1)S(1)}, bf16[128,2560]{1,0:T(8,128)(2,1)}, u32[]{:S(2)}) copy-start(bf16[128,2560]{1,0:T(8,128)(2,1)} %param.9) | copy-start | bytes 1966084
Sparse Core Ops, SparseCore 0:
  8.9 316.2 all-gather.3
  338.6 7.8 reduce-scatter.2
  417.7 242.2 all-gather.5
  667.7 15.1 reduce-scatter.4
where the time goes:
time: 697 us; the launch traced here: 695 us
  waiting for transfers between devices  431 us (62%)
  blocking collectives  108 us (15%)
  local copies, waits for them, and re-layouts  85.7 us (12%)
  matrix products  45.5 us (7%)
  between operations  14.1 us (2%)
  other arithmetic  8.88 us (1%)
    all_gather x1, waiting for transfers between devices, local(): lax.all_gather(w_qkv, 'ctx', axis=2, tiled=True)  318 us
    all_gather x1, waiting for transfers between devices, local(): lax.all_gather(own_cols, 'ctx', axis=1, tiled=True)  96.7 us
    dynamic_slice x1, local copies, waits for them, and re-layouts, local(): lax.dynamic_index_in_dim(split_cols, me_sub, 3, keepdims=False)  55.3 us
    all_gather x1, blocking collectives, local(): cur_keys = lax.all_gather(k_cur, ('ctx', 'sub'), axis=0, tiled=True)  30.2 us
    all_gather x1, blocking collectives, local(): cur_values = lax.all_gather(v_cur, ('ctx', 'sub'), axis=0, tiled=True)  27.9 us
    all_gather x1, blocking collectives, local(): old_values = lax.all_gather(prev_values, ('ctx', 'sub'), axis=0, tiled=True)  26.1 us
    all_gather x1, blocking collectives, local(): old_keys = lax.all_gather(k_prev, ('ctx', 'sub'), axis=0, tiled=True)  16.1 us
    reduce_scatter x1, waiting for transfers between devices, local(): lax.psum_scatter(summed.astype(jnp.bfloat16), 'head', scatter_dimension=1...  15.3 us
  transfers between devices with their start and end apart: 4, of which 3 were waited for; matrix products, arithmetic and copies ran while one was open for 17% of the time, Pallas kernels for 0%

commit v1 on v0

--- a/solution.py
+++ b/solution.py
@@ -42,12 +42,24 @@
     kv_dev = w_qkv.shape[1]
     me_ctx = lax.axis_index("ctx")
     me_sub = lax.axis_index("sub")
-    partial_value = jnp.einsum(
-        "td,dhn->thn",
-        hidden_in,
-        lax.all_gather(w_qkv, "ctx", axis=2, tiled=True),
-        preferred_element_type=jnp.float32,
-    )
+    response = lax.axis_index("ctx")
+    carry_in = lax.axis_size("ctx")
+    lower, h_now, near = (carry_in, response, w_qkv.shape[2])
+    long_array, partial_value = (w_qkv, None)
+    views = tuple(((nth, (nth + 1) % lower) for nth in range(lower)))
+    for b in range(lower):
+        small = (h_now - b) % lower
+        y1 = lax.ppermute(long_array, "ctx", views) if b < lower - 1 else None
+        known = jnp.einsum("td,dhn->thn", hidden_in, long_array, preferred_element_type=jnp.float32)
+        kept_arr = known.shape[2]
+        if partial_value is None:
+            partial_value = jnp.zeros(
+                (*known.shape[:2], lower * kept_arr, *known.shape[2 + 1 :]), known.dtype
+            )
+        partial_value = lax.dynamic_update_slice_in_dim(
+            partial_value, known, small * kept_arr, axis=2
+        )
+        long_array = y1
     joined = lax.psum_scatter(partial_value, "sub", scatter_dimension=0, tiled=True)
     joined = (joined + qkv_bias.astype(jnp.float32)[None]).reshape(tok_dev, kv_dev, G + 2, HD)
     owner_block = lookup(shard_blocks, me_ctx)

time: 697 us -> 684 us (0.981)
  waiting for transfers between devices: 431 us -> 399 us
  local copies, waits for them, and re-layouts: 85.7 us -> 101 us
    all_gather x1 -> x0, waiting for transfers between devices: 318 us -> none  [local(): lax.all_gather(w_qkv, 'ctx', axis=2, tiled=True)]
    ppermute x0 -> x3, waiting for transfers between devices: none -> 285 us  [local(): y1 = lax.ppermute(long_array, 'ctx', views) if b < lower - 1 else None]
    unnamed x0 -> x4, matrix products: none -> 14.5 us
    dot_general x1 -> x0, matrix products: 13.3 us -> none  [local(): jnp.einsum('td,dhn->thn', hidden_in, lax.all_gather(w_qkv, 'ctx', axis=2,...]
    dynamic_update_slice x0 -> x4, local copies, waits for them, and re-layouts: none -> 11.1 us  [local(): lax.dynamic_update_slice_in_dim(partial_value, known, small * kept_arr, a...]
  transfers between devices with their start and end apart: 4 -> 6, of which waited for: 3 -> 5; matrix products, arithmetic and copies ran while one was open for 17% -> 20% of each run, Pallas kernels for 0% -> 0%
where the time goes in v1:
time: 684 us; the launch traced here: 683 us
  waiting for transfers between devices  399 us (58%)
  blocking collectives  106 us (15%)
  local copies, waits for them, and re-layouts  101 us (15%)
  matrix products  46.7 us (7%)
  between operations  15.9 us (2%)
  other arithmetic  8.94 us (1%)
    ppermute x3, waiting for transfers between devices, local(): y1 = lax.ppermute(long_array, 'ctx', views) if b < lower - 1 else None  285 us
    all_gather x1, waiting for transfers between devices, local(): lax.all_gather(own_cols, 'ctx', axis=1, tiled=True)  97.8 us
    dynamic_slice x1, local copies, waits for them, and re-layouts, local(): lax.dynamic_index_in_dim(split_cols, me_sub, 3, keepdims=False)  55.3 us
    all_gather x1, blocking collectives, local(): cur_keys = lax.all_gather(k_cur, ('ctx', 'sub'), axis=0, tiled=True)  29.1 us
    all_gather x1, blocking collectives, local(): cur_values = lax.all_gather(v_cur, ('ctx', 'sub'), axis=0, tiled=True)  28.5 us
    all_gather x1, blocking collectives, local(): old_values = lax.all_gather(prev_values, ('ctx', 'sub'), axis=0, tiled=True)  24 us
    all_gather x1, blocking collectives, local(): old_keys = lax.all_gather(k_prev, ('ctx', 'sub'), axis=0, tiled=True)  17 us
    reduce_scatter x1, waiting for transfers between devices, local(): lax.psum_scatter(summed.astype(jnp.bfloat16), 'head', scatter_dimension=1...  15.6 us
  transfers between devices with their start and end apart: 6, of which 5 were waited for; matrix products, arithmetic and copies ran while one was open for 20% of the time, Pallas kernels for 0%

profile of v1, /device:TPU:0, one launch (start us, length us, event | category | flops | bytes accessed | tf_op | source)
XLA Modules:
  0.0 682.9 jit_solution(6855947114044422506)
XLA Ops:
  7.4 3.1 collective-permute-start
  10.4 101.2 %collective-permute-done = bf16[2560,4,224]{0,2,1:T(8,128)(2,1)S(1)} collective-permute-done((bf16[2560,4,224]{0,2,1:T(8,128)(2,1)}, bf16[2560,4,224]{0,2,1:T(8,128)(2,1)S(1)}, u32[]{:S(2)}, u32[]{:S(2)}) %collective-permute-start) | collective-permute-done | bytes 4587552 | tf_op jit(solution)/shard_map/ppermute | solution.py:52
  111.7 2.1 copy-done.3
  113.7 102.1 %collective-permute-done.1 = bf16[2560,4,224]{0,2,1:T(8,128)(2,1)} collective-permute-done((bf16[2560,4,224]{0,2,1:T(8,128)(2,1)S(1)}, bf16[2560,4,224]{0,2,1:T(8,128)(2,1)}, u32[]{:S(2)}, u32[]{:S(2)}) %collective-permute-start.1) | collective-permute-done | bytes 4587552 | tf_op jit(solution)/shard_map/ppermute | solution.py:52
  215.8 3.6 fusion.44
  219.8 2.4 dynamic_update_slice.12
  222.2 3.6 fusion.45
  226.0 2.3 dynamic_update_slice.13
  228.3 3.6 fusion.46
  232.2 3.2 dynamic_update_slice.14
  235.4 81.8 %collective-permute-done.2 = bf16[2560,4,224]{0,2,1:T(8,128)(2,1)} collective-permute-done((bf16[2560,4,224]{0,2,1:T(8,128)(2,1)}, bf16[2560,4,224]{0,2,1:T(8,128)(2,1)}, u32[]{:S(2)}, u32[]{:S(2)}) %collective-permute-start.2) | collective-permute-done | bytes 4587552 | tf_op jit(solution)/shard_map/ppermute | solution.py:52
  317.2 3.6 fusion.47
  321.1 3.2 dynamic_update_slice.15
  324.3 1.2 copy-done.2
  325.8 15.2 %reshape.509 = bf16[4,160,2,2,1280]{4,3,2,1,0:T(2,128)(2,1)} reshape(bf16[4,160,5120]{2,1,0:T(8,128)(2,1)} %param.12) | data formatting | bytes 13107200 | tf_op jit(solution)/shard_map/reshape | solution.py:161
  341.0 55.3 %dynamic-slice_reduce_fusion = bf16[4,160,2,1280]{3,2,1,0:T(2,128)(2,1)} fusion(bf16[4,160,2,2,1280]{4,3,2,1,0:T(2,128)(2,1)} %reshape.509, s32[]{:T(128)S(6)} %select_n.355), kind=kLoop, calls=%fused_computation.63 | loop fusion | bytes 6553604 | tf_op jit(solution)/shard_map/jit(dynamic_index_in_dim)/dynamic_slice | solution.py:162
  396.3 8.2 %reshape.510 = bf16[4,160,2560]{2,1,0:T(8,128)(2,1)} reshape(bf16[4,160,2,1280]{3,2,1,0:T(2,128)(2,1)} %dynamic-slice_reduce_fusion) | data formatting | bytes 6553600 | tf_op jit(solution)/shard_map/reshape | solution.py:162
  404.7 0.7 fusion.36
  406.2 0.4 multiply_cosine_fusion
  406.9 17.0 %all_gather.19 = bf16[512,4,128]{2,0,1:T(8,128)(2,1)S(1)} all-gather(bf16[64,4,128]{2,0,1:T(8,128)(2,1)S(1)} %pad_maximum_fusion.1), channel_id=1, replica_groups=mesh['groups'=2,'ctx'=4,'head'=2,'sub'=2] {'ctx','sub'}, dimensions={0}, use_global_device_ids=true | all-gather | bytes 589824 | tf_op jit(solution)/shard_map/all_gather | solution.py:138
  423.8 24.0 %all_gather.21 = bf16[512,4,128]{2,0,1:T(8,128)(2,1)} all-gather(bf16[64,4,128]{2,0,1:T(8,128)(2,1)S(1)} %copy.52), channel_id=1, replica_groups=mesh['groups'=2,'ctx'=4,'head'=2,'sub'=2] {'ctx','sub'}, dimensions={0}, use_global_device_ids=true | all-gather | bytes 589824 | tf_op jit(solution)/shard_map/all_gather | solution.py:139
  447.9 1.2 broadcast_add_fusion.1
  449.8 29.1 %all_gather.18 = bf16[512,4,128]{2,0,1:T(8,128)(2,1)} all-gather(bf16[64,4,128]{2,0,1:T(8,128)(2,1)S(1)} %pad_maximum_fusion), channel_id=1, replica_groups=mesh['groups'=2,'ctx'=4,'head'=2,'sub'=2] {'ctx','sub'}, dimensions={0}, use_global_device_ids=true | all-gather | bytes 589824 | tf_op jit(solution)/shard_map/all_gather | solution.py:136
  478.9 28.5 %all-gather = bf16[512,4,1,128]{3,2,0,1:T(2,128)(2,1)S(1)} all-gather(bf16[64,4,1,128]{3,2,0,1:T(2,128)(2,1)S(1)} %slice.97), channel_id=2, replica_groups=mesh['groups'=2,'ctx'=4,'head'=2,'sub'=2] {'ctx','sub'}, dimensions={0}, use_global_device_ids=true | all-gather | bytes 589824 | tf_op jit(solution)/shard_map/all_gather | solution.py:137
  507.5 1.1 subtract_convert_fusion
  508.6 0.4 maximum_bitcast_fusion.2
  509.0 0.4 copy.50
  509.5 0.4 maximum_bitcast_fusion.1
  509.8 0.4 copy.49
  510.3 0.4 maximum_bitcast_fusion
  510.7 0.4 copy.48
  511.2 34.2 %while.21 = (s32[]{:T(128)}, f32[4,320]{1,0:T(4,128)S(1)}, f32[4,320]{1,0:T(4,128)S(1)}, f32[4,320,128]{2,1,0:T(8,128)S(1)}, s32[4]{0:T(128)S(1)}, /*index=5*/s3...) while((s32[]{:T(128)}, f32[4,320]{1,0:T(4,128)S(1)}, ...), condition=%wide.region_8.9_spmd.clone, body=%wide.region_2.8_spmd.clone.sunk | while | flops 86380112 | bytes 6466017 | solution.py:153
  512.1 1.1 select_reduce_fusion.5
  513.2 0.3 fusion.73
  513.7 0.6 fusion.79
  514.3 1.2 convolution_add_fusion.3
  516.4 1.1 select_reduce_fusion.5
  518.0 0.6 fusion.79
  518.5 1.2 convolution_add_fusion.3
  520.7 1.1 select_reduce_fusion.5
  522.3 0.6 fusion.79
  522.8 1.2 convolution_add_fusion.3
  524.9 1.1 select_reduce_fusion.5
  526.5 0.6 fusion.79
  527.1 1.2 convolution_add_fusion.3
  529.2 1.1 select_reduce_fusion.5
  530.8 0.6 fusion.79
  531.4 1.2 convolution_add_fusion.3
  533.5 1.1 select_reduce_fusion.5
  535.1 0.6 fusion.79
  535.7 1.2 convolution_add_fusion.3
  537.8 1.1 select_reduce_fusion.5
  539.4 0.6 fusion.79
  539.9 1.2 convolution_add_fusion.3
  542.0 1.1 select_reduce_fusion.5
  543.6 0.6 fusion.79
  544.2 1.2 convolution_add_fusion.3
  546.0 0.4 reshape.508
  546.4 2.3 all_gather.22
  548.7 97.8 %all-gather.3.cloned.1.call-done = bf16[4,640,2560]{2,1,0:T(8,128)(2,1)} async-done(((bf16[4,160,2560]{2,1,0:T(8,128)(2,1)}), bf16[4,640,2560]{2,1,0:T(8,128)(2,1)}) %all-gather.3.cloned.1.call-update) | async-done | bytes 13107216 | tf_op jit(solution)/shard_map/all_gather | solution.py:169
  646.5 7.5 %fusion.35 = bf16[128,2560]{1,0:T(8,128)(2,1)} fusion(bf16[128,4,640]{2,0,1:T(8,128)(2,1)S(1)} %all_gather.22, bf16[4,640,2560]{2,1,0:T(8,128)(2,1)} %all-gather.3.cloned.1.call-done), kind=kOutput, calls=%fused_computation.65 | convolution fusion | flops 1678049280 | bytes 14417920 | tf_op jit(solution)/shard_map/thn,hnd->td/dot_general | solution.py:166
  654.0 15.6 %reduce-scatter.5.cloned.1.call-done = bf16[128,1280]{1,0:T(8,128)(2,1)} async-done(((bf16[128,2560]{1,0:T(8,128)(2,1)}), bf16[128,1280]{1,0:T(8,128)(2,1)}) %reduce-scatter.5.cloned.1.call-update) | async-done | bytes 327696 | tf_op jit(solution)/shard_map/reduce_scatter | solution.py:172
  669.6 5.0 all_to_all.19
  674.7 0.7 copy.62
  (180 shorter events, 11.9 us)
Async XLA Ops:
  7.4 208.4 %copy-start = (bf16[128,2560]{1,0:T(8,128)(2,1)S(1)}, bf16[128,2560]{1,0:T(8,128)(2,1)}, u32[]{:S(2)}) copy-start(bf16[128,2560]{1,0:T(8,128)(2,1)} %param.9) | copy-start | bytes 1966084
  7.4 440.5 %reduce-scatter.3.cloned.1.call-start = ((), (), s32[]{:S(2)}) async-start(), calls=%async_computation.3 | async-start | bytes 2752512 | tf_op jit(solution)/shard_map/reduce_scatter | solution.py:63
  7.4 104.3 %collective-permute-start = (bf16[2560,4,224]{0,2,1:T(8,128)(2,1)}, bf16[2560,4,224]{0,2,1:T(8,128)(2,1)S(1)}, u32[]{:S(2)}, u32[]{:S(2)}) collective-permute-start(bf16[2560,4,224]{0,2,1:T(8,128)(2,1)} %param.10), channel_id=1, source_target_pairs={{0,4},{4,8},{8,12},{12,0},{1,5},{5,9},{9,13},{13,1},{2,6},{6,10},{... | collective-permute-start | bytes 13762568 | tf_op jit(solution)/shard_map/ppermute | solution.py:52
  111.7 2.1 copy-start.3
  113.7 102.1 %collective-permute-start.1 = (bf16[2560,4,224]{0,2,1:T(8,128)(2,1)S(1)}, bf16[2560,4,224]{0,2,1:T(8,128)(2,1)}, u32[]{:S(2)}, u32[]{:S(2)}) collective-permute-start(bf16[2560,4,224]{0,2,1:T(8,128)(2,1)S(1)} %collective-permute-done), channel_id=1, source_target_pairs={{0,4},{4,8},{8,12},{12,0},{1,5},{5,9},{9,13},{13,1},{2,6},{6,10},{... | collective-permute-start | bytes 13762568 | tf_op jit(solution)/shard_map/ppermute | solution.py:52
  215.8 101.4 %collective-permute-start.2 = (bf16[2560,4,224]{0,2,1:T(8,128)(2,1)}, bf16[2560,4,224]{0,2,1:T(8,128)(2,1)}, u32[]{:S(2)}, u32[]{:S(2)}) collective-permute-start(bf16[2560,4,224]{0,2,1:T(8,128)(2,1)} %collective-permute-done.1), channel_id=1, source_target_pairs={{0,4},{4,8},{8,12},{12,0},{1,5},{5,9},{9,13},{13,1},{2,6},{6,10},{... | collective-permute-start | bytes 13762568 | tf_op jit(solution)/shard_map/ppermute | solution.py:52
  324.3 1.2 copy-start.2
  325.6 320.9 %all-gather.3.cloned.1.call-start = ((), (), s32[]{:S(2)}) async-start(), calls=%async_computation.4 | async-start | bytes 16384000 | tf_op jit(solution)/shard_map/all_gather | solution.py:169
  396.3 8.3 %copy-start.7 = (s32[4]{0:T(128)S(1)}, s32[4]{0:T(128)}, u32[]{:S(2)}) copy-start(s32[4]{0:T(128)} %param.15) | copy-start | bytes 52
  396.3 9.8 %copy-start.6 = (bf16[4,896]{1,0:T(4,128)(2,1)S(1)}, bf16[4,896]{1,0:T(4,128)(2,1)}, u32[]{:S(2)}) copy-start(bf16[4,896]{1,0:T(4,128)(2,1)} %param.11) | copy-start | bytes 21508
  396.3 9.8 %copy-start.5 = (bf16[64,4,128]{2,1,0:T(4,128)(2,1)S(1)}, bf16[64,4,128]{2,1,0:T(4,128)(2,1)}, u32[]{:S(2)}) copy-start(bf16[64,4,128]{2,1,0:T(4,128)(2,1)} %param.14) | copy-start | bytes 196612
  396.3 9.9 %copy-start.4 = (bf16[64,4,128]{2,1,0:T(4,128)(2,1)S(1)}, bf16[64,4,128]{2,1,0:T(4,128)(2,1)}, u32[]{:S(2)}) copy-start(bf16[64,4,128]{2,1,0:T(4,128)(2,1)} %param.13) | copy-start | bytes 196612
  404.6 265.1 %reduce-scatter.5.cloned.1.call-start = ((), (), s32[]{:S(2)}) async-start(), calls=%async_computation.5 | async-start | bytes 983040 | tf_op jit(solution)/shard_map/reduce_scatter | solution.py:172
  646.5 28.9 %copy-start.1 = (bf16[128,2560]{1,0:T(8,128)(2,1)S(1)}, bf16[128,2560]{1,0:T(8,128)(2,1)}, u32[]{:S(2)}) copy-start(bf16[128,2560]{1,0:T(8,128)(2,1)} %param.9) | copy-start | bytes 1966084
Sparse Core Ops, SparseCore 0:
  325.7 7.1 reduce-scatter.2
  654.2 15.4 reduce-scatter.4
Sparse Core Ops, SparseCore 1:
  404.7 241.8 all-gather.2
